TPU v7x, 32 devices: a whole 2x2x4 slice. The times are simulated.
32 devices in a mesh: seq: 8 (over z, x), wa: 4 (over y, core).
Axes of the slice: x: 2, y: 2, z: 4, core: 2. Of those that a mesh axis runs over, the one named last changes fastest.
Arguments:
- tokens: bfloat16 [8, 1024, 2048], P('wa', 'seq'), may hold values from -6 to 6
- lengths: int32 [8], P('wa'), may hold values from 256 to 1024, as said below
- norm_gain: float32 [2048], replicated, may hold values from 0.25 to 1.75
- in_weight: bfloat16 [2048, 8512], P('wa'), may hold values from -0.125 to 0.125
- conv_weight: float32 [4, 4352], replicated, may hold values from -3 to 3
- conv_bias: float32 [4352], replicated, may hold values from -1.8 to 1.8
- dt_bias: float32 [64], replicated, may hold values from -8 to -2
- a_log: float32 [64], replicated, may hold values from 0 to 2.77
- skip_gain: float32 [64], replicated, may hold values from 0.5 to 2
- out_gain: float32 [4096], replicated, may hold values from 0.25 to 1.75
- out_weight: bfloat16 [4096, 2048], P('wa'), may hold values from -0.09375 to 0.09375
- cotangent: bfloat16 [8, 1024, 2048], P('wa', 'seq'), may hold values from -6 to 6
Outputs:
- mixed_out: bfloat16 [8, 1024, 2048], P('wa', 'seq')
- grad_tokens: float32 [8, 1024, 2048], P('wa', 'seq')
- grad_norm_gain: float32 [2048], replicated
- grad_in_weight: float32 [2048, 8512], P('wa')
- grad_conv_weight: float32 [4, 4352], replicated
- grad_conv_bias: float32 [4352], replicated
- grad_dt_bias: float32 [64], replicated
- grad_a_log: float32 [64], replicated
- grad_skip: float32 [64], replicated
- grad_out_gain: float32 [4096], replicated
- grad_out_weight: float32 [4096, 2048], P('wa')
Inputs may be any that keep to these rules, and one draw needn't show every extreme that they name: `lengths`: each sequence's used slots come first; in each group of 2 sequences laid out on one index of wa one sequence is full.
All inputs are finite; a program needn't handle non-finite values.
Results may differ from a plain program's by a relative error of at most 0.012.
Values may be sent and summed in bfloat16 or wider, within the bound.
A program may use at most 384 MiB of HBM per device.

v0:
```python
import jax
import jax.numpy as jnp
from jax import lax
from jax.sharding import PartitionSpec as P

KW = 4
BLOCK_LEN = 256
EPS = 1e-05
HIGH = lax.Precision.HIGHEST


def row_scale(values):
    return lax.rsqrt(jnp.mean(values * values, axis=-1, keepdims=True) + EPS)


def norm_backward(values, row_scales, gain_vec, grad_out):
    weighted = grad_out * gain_vec
    grad_gain = jnp.sum(grad_out * values * row_scales, axis=0)
    grad_values = row_scales * weighted - values * row_scales**3 * jnp.mean(
        weighted * values, axis=-1, keepdims=True
    )
    return (grad_values, grad_gain)


def block_chain(x_heads, dt_vals, rates, b_rows, c_rows, block_len):
    seqs_here, length, head_total, head_size = x_heads.shape
    block_count = length // block_len
    states_dim = b_rows.shape[-1]
    x_blocks = x_heads.reshape(seqs_here, block_count, block_len, head_total, head_size)
    dt_blocks = jnp.swapaxes(dt_vals.reshape(seqs_here, block_count, block_len, head_total), 2, 3)
    rate_blocks = jnp.swapaxes(rates.reshape(seqs_here, block_count, block_len, head_total), 2, 3)
    b_blocks = b_rows.reshape(seqs_here, block_count, block_len, states_dim)
    c_blocks = c_rows.reshape(seqs_here, block_count, block_len, states_dim)
    cumulative = jnp.cumsum(rate_blocks, axis=-1)
    causal_mask = jnp.arange(block_len)[:, None] >= jnp.arange(block_len)[None, :]
    log_decay = cumulative[..., :, None] - cumulative[..., None, :]
    decay_matrix = jnp.where(causal_mask, jnp.exp(jnp.where(causal_mask, log_decay, 0.0)), 0.0)
    scores = jnp.einsum("sbin,sbjn->sbij", c_blocks, b_blocks, precision=HIGH)
    weights = scores[:, :, None] * decay_matrix * dt_blocks[..., None, :]
    inner_part = jnp.einsum("sbhij,sbjhp->sbihp", weights, x_blocks, precision=HIGH)
    tail_decay = jnp.exp(cumulative[..., -1:] - cumulative) * dt_blocks
    block_states = jnp.einsum(
        "sbhj,sbjhp,sbjn->sbhpn", tail_decay, x_blocks, b_blocks, precision=HIGH
    )
    block_decay = jnp.exp(cumulative[..., -1])

    def carry_step(carry_state, pieces):
        decay_now, state_now = pieces
        return (decay_now[..., None, None] * carry_state + state_now, carry_state)

    start_state = jnp.zeros((seqs_here, head_total, head_size, states_dim), jnp.float32)
    final_state, entering = lax.scan(
        carry_step, start_state, (jnp.moveaxis(block_decay, 1, 0), jnp.moveaxis(block_states, 1, 0))
    )
    entering = jnp.moveaxis(entering, 0, 1)
    carried = jnp.swapaxes(jnp.exp(cumulative), 2, 3)[..., None] * jnp.einsum(
        "sbin,sbhpn->sbihp", c_blocks, entering, precision=HIGH
    )
    output = (inner_part + carried).reshape(seqs_here, length, head_total, head_size)
    return (output, final_state)


def mixer_front(
    extended, dt_raw, conv_w, conv_b, bias_part, log_rates, x_width, state_size, head_size
):
    seqs_here = extended.shape[0]
    length = extended.shape[1] - (KW - 1)
    conv_sum = conv_b
    for offset in range(KW):
        conv_sum = conv_sum + conv_w[offset] * extended[:, offset : offset + length]
    activated = jax.nn.silu(conv_sum)
    x_heads = activated[..., :x_width].reshape(seqs_here, length, x_width // head_size, head_size)
    b_rows = activated[..., x_width : x_width + state_size]
    c_rows = activated[..., x_width + state_size :]
    dt_vals = jax.nn.softplus(dt_raw + bias_part)
    rates = -jnp.exp(log_rates) * dt_vals
    block_len = min(BLOCK_LEN, length)
    y_local, local_state = block_chain(x_heads, dt_vals, rates, b_rows, c_rows, block_len)
    running = jnp.exp(jnp.cumsum(rates, axis=1))
    total_decay = running[:, -1]
    return (y_local, local_state, total_decay, x_heads, c_rows, running)


def mixer_finish(y_local, x_heads, gate_part, skip_part):
    y_heads = y_local + skip_part[:, None] * x_heads
    seqs_here, length = (y_heads.shape[0], y_heads.shape[1])
    return y_heads.reshape(seqs_here, length, -1) * jax.nn.silu(gate_part)


def body(
    tokens,
    lengths,
    norm_gain,
    in_weight,
    conv_weight,
    conv_bias,
    dt_bias,
    a_log,
    skip_gain,
    out_gain,
    out_weight,
    cotangent,
):
    seqs_here, slot_rows, width = tokens.shape
    row_count = seqs_here * slot_rows
    inner_width = out_gain.shape[0]
    channels = conv_bias.shape[0]
    state_size = (channels - inner_width) // 2
    head_count = dt_bias.shape[0]
    head_size = inner_width // head_count
    seq_devices = lax.axis_size("seq")
    seq_index = lax.axis_index("seq")
    positions = seq_index * slot_rows + jnp.arange(slot_rows)
    valid_rows = (positions[None, :] < lengths[:, None]).astype(jnp.float32).reshape(row_count, 1)
    flat_tokens = tokens.reshape(row_count, width).astype(jnp.float32)
    in_scale = row_scale(flat_tokens)
    normed = (flat_tokens * in_scale * norm_gain).astype(jnp.bfloat16)
    columns = normed
    projected = jnp.dot(
        columns,
        lax.all_gather(in_weight, "wa", axis=0, tiled=True),
        preferred_element_type=jnp.float32,
    ).astype(jnp.bfloat16)
    gate_part = projected[:, :inner_width].reshape(seqs_here, slot_rows, inner_width)
    conv_in = projected[:, inner_width : inner_width + channels].reshape(
        seqs_here, slot_rows, channels
    )
    dt_raw = projected[:, inner_width + channels :].reshape(seqs_here, slot_rows, head_count)
    local_heads = head_count // seq_devices
    local_width = local_heads * head_size
    channel_start = seq_index * local_width
    head_start = seq_index * local_heads
    gate_heads, x_heads_in, dt_heads = (
        lax.all_to_all(gate_part, "seq", split_axis=2, concat_axis=1, tiled=True),
        lax.all_to_all(conv_in[..., :inner_width], "seq", split_axis=2, concat_axis=1, tiled=True),
        lax.all_to_all(dt_raw, "seq", split_axis=2, concat_axis=1, tiled=True),
    )
    bc_heads = lax.all_gather(conv_in[..., inner_width:], "seq", axis=1, tiled=True)
    joined = jnp.concatenate([x_heads_in, bc_heads], axis=2).astype(jnp.float32)
    extended = jnp.concatenate(
        [jnp.zeros((seqs_here, KW - 1, joined.shape[2]), jnp.float32), joined], axis=1
    )
    conv_local = jnp.concatenate(
        [
            lax.dynamic_slice_in_dim(conv_weight, channel_start, local_width, 1),
            conv_weight[:, inner_width:],
        ],
        axis=1,
    )
    bias_local = jnp.concatenate(
        [
            lax.dynamic_slice_in_dim(conv_bias, channel_start, local_width, 0),
            conv_bias[inner_width:],
        ],
        axis=0,
    )
    shift_local = lax.dynamic_slice_in_dim(dt_bias, head_start, local_heads, 0)
    rates_local = lax.dynamic_slice_in_dim(a_log, head_start, local_heads, 0)
    skip_local = lax.dynamic_slice_in_dim(skip_gain, head_start, local_heads, 0)

    def front_fn(extended_in, dt_in, conv_w, conv_b, bias_part, log_rates):
        return mixer_front(
            extended_in,
            dt_in,
            conv_w,
            conv_b,
            bias_part,
            log_rates,
            local_width,
            state_size,
            head_size,
        )

    front_out, front_pull = jax.vjp(
        front_fn,
        extended,
        dt_heads.astype(jnp.float32),
        conv_local,
        bias_local,
        shift_local,
        rates_local,
    )
    y_local, local_state, total_decay, x_heads, c_rows, running = front_out

    def finish_fn(y_in, x_in, gate_in, skip_in):
        return mixer_finish(y_in, x_in, gate_in, skip_in)

    gated_heads, finish_pull = jax.vjp(
        finish_fn, y_local, x_heads, gate_heads.astype(jnp.float32), skip_local
    )
    gated_tok = lax.all_to_all(
        gated_heads.astype(jnp.bfloat16), "seq", split_axis=1, concat_axis=2, tiled=True
    )
    gated_rows = gated_tok.reshape(row_count, inner_width).astype(jnp.float32)
    out_scale = row_scale(gated_rows)
    normed_out = (gated_rows * out_scale * out_gain).astype(jnp.bfloat16)
    columns = normed_out
    branch = jnp.dot(
        columns,
        lax.all_gather(out_weight, "wa", axis=0, tiled=True),
        preferred_element_type=jnp.float32,
    )
    mixed_out = (flat_tokens + valid_rows * branch).astype(jnp.bfloat16).reshape(tokens.shape)
    cot_rows = cotangent.reshape(row_count, width)
    branch_grad = cot_rows * valid_rows.astype(jnp.bfloat16)
    columns = normed_out
    out_weight_grad = lax.psum_scatter(
        lax.dot_general(
            columns, branch_grad, (((0,), (0,)), ((), ())), preferred_element_type=jnp.float32
        ),
        "wa",
        scatter_dimension=0,
        tiled=True,
    )
    normed_out_grad = lax.dot_general(
        branch_grad,
        lax.all_gather(out_weight, "wa", axis=0, tiled=True),
        (((1,), (1,)), ((), ())),
        preferred_element_type=jnp.float32,
    )
    gated_grad, out_gain_grad = norm_backward(gated_rows, out_scale, out_gain, normed_out_grad)
    gated_grad = gated_grad.astype(jnp.bfloat16).reshape(seqs_here, slot_rows, inner_width)
    grad_heads = lax.all_to_all(gated_grad, "seq", split_axis=2, concat_axis=1, tiled=True).astype(
        jnp.float32
    )
    y_grad, x_grad, gate_grad, skip_part_grad = finish_pull(grad_heads)
    front_grads = front_pull(
        (
            y_grad,
            jnp.zeros_like(local_state),
            jnp.zeros_like(total_decay),
            x_grad,
            jnp.zeros_like(c_rows),
            jnp.zeros_like(running),
        )
    )
    extended_grad, dt_grad, conv_w_grad, conv_b_grad, shift_grad, rates_grad = front_grads
    conv_heads_grad = extended_grad[:, KW - 1 :]
    gate_back, x_back, dt_back = (
        lax.all_to_all(
            gate_grad.astype(jnp.bfloat16), "seq", split_axis=1, concat_axis=2, tiled=True
        ),
        lax.all_to_all(
            conv_heads_grad[..., :local_width].astype(jnp.bfloat16),
            "seq",
            split_axis=1,
            concat_axis=2,
            tiled=True,
        ),
        lax.all_to_all(
            dt_grad.astype(jnp.bfloat16), "seq", split_axis=1, concat_axis=2, tiled=True
        ),
    )
    bc_back = lax.psum_scatter(
        conv_heads_grad[..., local_width:].astype(jnp.bfloat16),
        "seq",
        scatter_dimension=1,
        tiled=True,
    )
    proj_grad = jnp.concatenate([gate_back, x_back, bc_back, dt_back], axis=2)
    x_taps = lax.dynamic_update_slice_in_dim(
        jnp.zeros((KW, inner_width), jnp.float32), conv_w_grad[:, :local_width], channel_start, 1
    )
    conv_weight_grad = jnp.concatenate([x_taps, conv_w_grad[:, local_width:]], axis=1)
    x_bias = lax.dynamic_update_slice_in_dim(
        jnp.zeros((inner_width,), jnp.float32), conv_b_grad[:local_width], channel_start, 0
    )
    conv_bias_grad = jnp.concatenate([x_bias, conv_b_grad[local_width:]], axis=0)
    head_zeros = jnp.zeros((head_count,), jnp.float32)
    dt_bias_grad = lax.dynamic_update_slice_in_dim(head_zeros, shift_grad, head_start, 0)
    a_log_grad = lax.dynamic_update_slice_in_dim(head_zeros, rates_grad, head_start, 0)
    skip_grad = lax.dynamic_update_slice_in_dim(head_zeros, skip_part_grad, head_start, 0)
    proj_rows = proj_grad.reshape(row_count, proj_grad.shape[2])
    columns = normed
    in_weight_grad = lax.psum_scatter(
        lax.dot_general(
            columns, proj_rows, (((0,), (0,)), ((), ())), preferred_element_type=jnp.float32
        ),
        "wa",
        scatter_dimension=0,
        tiled=True,
    )
    normed_grad = lax.dot_general(
        proj_rows,
        lax.all_gather(in_weight, "wa", axis=0, tiled=True),
        (((1,), (1,)), ((), ())),
        preferred_element_type=jnp.float32,
    )
    token_grad, norm_gain_grad = norm_backward(flat_tokens, in_scale, norm_gain, normed_grad)
    token_grad = token_grad + cot_rows.astype(jnp.float32)
    in_weight_grad, out_weight_grad = lax.psum((in_weight_grad, out_weight_grad), "seq")
    small_grads = lax.psum(
        (
            norm_gain_grad,
            conv_weight_grad,
            conv_bias_grad,
            dt_bias_grad,
            a_log_grad,
            skip_grad,
            out_gain_grad,
        ),
        ("seq", "wa"),
    )
    return (
        mixed_out,
        token_grad.reshape(tokens.shape),
        small_grads[0],
        in_weight_grad,
        small_grads[1],
        small_grads[2],
        small_grads[3],
        small_grads[4],
        small_grads[5],
        small_grads[6],
        out_weight_grad,
    )


def solution(mesh):
    placed = (
        P("wa", "seq", None),
        P("wa"),
        P(),
        P("wa", None),
        P(),
        P(),
        P(),
        P(),
        P(),
        P(),
        P("wa", None),
        P("wa", "seq", None),
    )
    return jax.shard_map(
        body,
        mesh=mesh,
        in_specs=placed,
        out_specs=(
            P("wa", "seq", None),
            P("wa", "seq", None),
            P(),
            P("wa", None),
            P(),
            P(),
            P(),
            P(),
            P(),
            P(),
            P("wa", None),
        ),
        check_vma=False,
    )
```

profile of v0, /device:TPU:0, one launch (start us, length us, event | category | flops | bytes accessed | tf_op | source)
XLA Modules:
  0.0 2436.3 jit_solution(2501192697912139225)
XLA Ops:
  10.1 213.5 %all-gather.4.cloned.1.call-done = bf16[2048,8512]{0,1:T(8,128)(2,1)} async-done(((bf16[512,8512]{0,1:T(8,128)(2,1)}), bf16[2048,8512]{0,1:T(8,128)(2,1)}) %all-gather.4.cloned.1.call-update) | async-done | bytes 34865168 | tf_op jit(solution)/shard_map/all_gather | solution.py:121
  223.6 15.1 convolution_convert_fusion
  277.8 43.5 %all-to-all-done = bf16[2,128,4096]{1,0,2:T(2,128)(2,1)S(1)} async-done(((bf16[2,128,4096]{1,0,2:T(2,128)(2,1)}), bf16[2,128,4096]{1,0,2:T(2,128)(2,1)S(1)}, u32[]{:S(2)}, u32[]{:S(2)}) %all-to-all-start) | async-done | bytes 2097184 | tf_op jit(solution)/shard_map/all_to_all | solution.py:135
  334.6 7.5 fusion.24
  376.8 19.7 bitcast_add_fusion.3
  433.1 43.9 %all-to-all-done.3 = bf16[2,1024,512]{2,0,1:T(2,128)(2,1)} async-done(((bf16[2,1024,512]{2,0,1:T(2,128)(2,1)}), bf16[2,1024,512]{2,0,1:T(2,128)(2,1)}, u32[]{:S(2)}, u32[]{:S(2)}) %all-to-all-start.3) | async-done | bytes 2097184 | tf_op jit(solution)/shard_map/all_to_all | solution.py:191
  495.5 14.9 multiply_reduce_fusion.7
  527.2 6.7 copy.494
  540.0 35.0 %all-to-all-done.4 = bf16[2,128,4096]{1,0,2:T(2,128)(2,1)} async-done(((bf16[2,128,4096]{1,0,2:T(2,128)(2,1)}), bf16[2,128,4096]{1,0,2:T(2,128)(2,1)}, u32[]{:S(2)}, u32[]{:S(2)}) %all-to-all-start.4) | async-done | bytes 2097184 | tf_op jit(solution)/shard_map/all_to_all | solution.py:223
  596.0 29.8 %fusion.9 = (f32[2,4,8,256]{3,2,1,0:T(8,128)S(1)}, f32[2,4,8,256]{3,2,1,0:T(8,128)S(1)}, f32[2,4,8,256]{3,2,1,0:T(8,128)}, f32[2,4,256,256]{3,2,1,0:T(8,128)}) fusion(f32[2,4,8,256]{3,2,1,0:T(8,128)S(1)} %get-tuple-element.439, f32[2,4,8,256]{3,2,1,0:T(8,128)S(1)} %get-tuple-element.437, f32[2,4,256,256]{3,2,1,0:T(8,128)S(1)} %copy-done.32, ...), kind=kOutput, calls=%fused_computation.21 | convolution fusion | flops 3283566592 | bytes 12976128 | tf_op jit(solution)/shard_map/transpose(jvp(sbhij,sbjhp->sbihp))/dot_general | solution.py:40
  631.0 7.7 fusion.90
  640.4 8.9 while.35
  649.3 10.8 fusion.85
  664.3 15.5 bitcast_add_fusion.2
  704.5 10.8 multiply_reduce_fusion.8
  716.6 10.7 multiply_reduce_fusion.4
  751.6 13.3 fusion.136
  771.0 19.8 reduce-window.34
  792.0 19.8 reduce-window.36
  817.8 16.8 add_convert_fusion
  836.9 6.7 copy.517
  853.6 44.1 %all-to-all-done.6 = bf16[2,1024,512]{2,0,1:T(2,128)(2,1)} async-done(((bf16[2,1024,512]{2,0,1:T(2,128)(2,1)}), bf16[2,1024,512]{2,0,1:T(2,128)(2,1)}, u32[]{:S(2)}, u32[]{:S(2)}) %all-to-all-start.6) | async-done | bytes 2097184 | tf_op jit(solution)/shard_map/all_to_all | solution.py:243
  907.8 42.0 %all-to-all-done.5 = bf16[2,1024,512]{2,0,1:T(2,128)(2,1)} async-done(((bf16[2,1024,512]{2,0,1:T(2,128)(2,1)}), bf16[2,1024,512]{2,0,1:T(2,128)(2,1)}, u32[]{:S(2)}, u32[]{:S(2)}) %all-to-all-start.5) | async-done | bytes 2097184 | tf_op jit(solution)/shard_map/all_to_all | solution.py:240
  954.8 28.3 %fusion.95 = f32[2048,8512]{0,1:T(8,128)} fusion(bf16[256,2048]{1,0:T(8,128)(2,1)} %copy-done.29, bf16[256,64]{1,0:T(8,128)(2,1)S(1)} %copy.528, bf16[256,256]{1,0:T(8,128)(2,1)S(1)} %bitcast.400, bf16[256,4096]{1,0:T(8,128)(2,1)S(1)} %bitcast.377, bf16[256,4096]{1,0:T(8,128)(2,1)} %bitcast.379), kind=kOutput, calls=%fused_computation.140 | convolution fusion | flops 8942911488 | bytes 75137024 | tf_op jit(solution)/shard_map/dot_general | solution.py:276
  984.6 59.7 %reduce-scatter.8.cloned.1.call-done = f32[1024,2048]{1,0:T(8,128)} async-done(((f32[4096,2048]{1,0:T(8,128)}), f32[1024,2048]{1,0:T(8,128)}) %reduce-scatter.8.cloned.1.call-update) | async-done | bytes 8388624 | tf_op jit(solution)/shard_map/reduce_scatter | solution.py:207
  1044.3 471.0 %reduce-scatter.6.cloned.1.call-done = f32[512,8512]{0,1:T(8,128)} async-done(((f32[2048,8512]{0,1:T(8,128)}), f32[512,8512]{0,1:T(8,128)}) %reduce-scatter.6.cloned.1.call-update) | async-done | bytes 17432592 | tf_op jit(solution)/shard_map/reduce_scatter | solution.py:275
  1516.6 12.6 fusion.49
  1530.5 18.1 fusion.58
  1548.7 40.5 %all-reduce.14 = (f32[2048]{0:T(1024)}, f32[4352]{0:T(1024)}, f32[64]{0:T(128)}, f32[64]{0:T(128)}, f32[64]{0:T(128)}, /*index=5*/f32[4096]{0:T(1024)}) all-reduce(f32[2048]{0:T(1024)S(1)} %get-tuple-element.389, f32[4352]{0:T(1024)S(1)} %pad_maximum_fusion.4, ...), channel_id=1, replica_groups=mesh['seq'=8,'wa'=4] {'seq','wa'}, use_global_device_ids=true, to_apply=%region_25.26 | all-reduce | flops 10688 | bytes 85504 | tf_op jit(solution)/shard_map/psum | solution.py:292
  1592.8 46.6 %all-reduce.19.cloned.1.call-done = f32[4,4352]{1,0:T(4,128)} async-done(((f32[4,4352]{1,0:T(4,128)}), f32[4,4352]{1,0:T(4,128)}) %all-reduce.19.cloned.1.call-update) | async-done | bytes 69648 | tf_op jit(solution)/shard_map/psum | solution.py:292
  1639.4 772.4 %all-reduce.21.cloned.1.call-done = (f32[512,8512]{0,1:T(8,128)}, f32[1024,2048]{1,0:T(8,128)}) async-done(((f32[512,8512]{0,1:T(8,128)}, f32[1024,2048]{1,0:T(8,128)}), (f32[512,8512]{0,1:T(8,128)}, f32[1024,2048]{1,0:T(8,128)})) %all-reduce.21.cloned.1.call-update) | async-done | bytes 25821200 | tf_op jit(solution)/shard_map/psum | solution.py:291
  2411.8 13.4 copy.711
  (397 shorter events, 314.9 us)
Async XLA Ops:
  7.2 216.4 %all-gather.4.cloned.1.call-start = ((), (), s32[]{:S(2)}) async-start(), calls=%async_computation.11 | async-start | bytes 43581440 | tf_op jit(solution)/shard_map/all_gather | solution.py:121
  7.9 323.9 %all-gather.6.cloned.1.call-start = ((), (), s32[]{:S(2)}) async-start(), calls=%async_computation.12 | async-start | bytes 1179648 | tf_op jit(solution)/shard_map/all_gather | solution.py:138
  10.1 228.5 %copy-start.29 = (bf16[256,2048]{1,0:T(8,128)(2,1)}, bf16[256,2048]{1,0:T(8,128)(2,1)S(1)}, u32[]{:S(2)}) copy-start(bf16[256,2048]{1,0:T(8,128)(2,1)S(1)} %fusion.52) | copy-start | bytes 3145732
  247.5 248.0 %all-gather.8.cloned.1.call-start = ((), (), s32[]{:S(2)}) async-start(), calls=%async_computation.13 | async-start | bytes 20971520 | tf_op jit(solution)/shard_map/all_gather | solution.py:200
  248.9 12.2 all-to-all-start.1
  261.1 60.2 %all-to-all-start = ((bf16[2,128,4096]{1,0,2:T(2,128)(2,1)}), bf16[2,128,4096]{1,0,2:T(2,128)(2,1)S(1)}, u32[]{:S(2)}, u32[]{:S(2)}) async-start(bf16[2,128,4096]{1,0,2:T(2,128)(2,1)} %slice.142), calls=%async_computation | async-start | bytes 4194304 | tf_op jit(solution)/shard_map/all_to_all | solution.py:135
  265.1 146.7 %copy-start.52 = (f32[512]{0:T(512)}, f32[512]{0:T(512)S(1)}, u32[]{:S(2)}) copy-start(f32[512]{0:T(512)S(1)} %mul.518) | copy-start | bytes 6148
  265.2 69.3 %copy-start.41 = (f32[768]{0:T(1024)}, f32[768]{0:T(1024)S(1)}, u32[]{:S(2)}) copy-start(f32[768]{0:T(1024)S(1)} %get-tuple-element.391) | copy-start | bytes 9220
  265.2 69.3 %copy-start.43 = (f32[768]{0:T(1024)}, f32[768]{0:T(1024)S(1)}, u32[]{:S(2)}) copy-start(f32[768]{0:T(1024)S(1)} %get-tuple-element.392) | copy-start | bytes 9220
  265.2 69.3 %copy-start.45 = (f32[768]{0:T(1024)}, f32[768]{0:T(1024)S(1)}, u32[]{:S(2)}) copy-start(f32[768]{0:T(1024)S(1)} %get-tuple-element.393) | copy-start | bytes 9220
  265.2 69.3 %copy-start.47 = (f32[768]{0:T(1024)}, f32[768]{0:T(1024)S(1)}, u32[]{:S(2)}) copy-start(f32[768]{0:T(1024)S(1)} %get-tuple-element.394) | copy-start | bytes 9220
  277.6 50.9 %copy-start.36 = (f32[2,4,8]{2,1,0:T(4,128)}, f32[2,4,8]{2,1,0:T(4,128)S(1)}, u32[]{:S(2)}) copy-start(f32[2,4,8]{2,1,0:T(4,128)S(1)} %slice_reduce_fusion.2) | copy-start | bytes 772
  321.3 85.9 %all-to-all-start.2 = ((bf16[2,128,4096]{1,0,2:T(2,128)(2,1)}), bf16[2,128,4096]{1,0,2:T(2,128)(2,1)}, u32[]{:S(2)}, u32[]{:S(2)}) async-start(bf16[2,128,4096]{1,0,2:T(2,128)(2,1)} %reshape.388), calls=%async_computation.2 | async-start | bytes 4194304 | tf_op jit(solution)/shard_map/all_to_all | solution.py:134
  424.1 53.0 %all-to-all-start.3 = ((bf16[2,1024,512]{2,0,1:T(2,128)(2,1)}), bf16[2,1024,512]{2,0,1:T(2,128)(2,1)}, u32[]{:S(2)}, u32[]{:S(2)}) async-start(bf16[2,1024,512]{2,0,1:T(2,128)(2,1)} %copy.495), calls=%async_computation.3 | async-start | bytes 4194304 | tf_op jit(solution)/shard_map/all_to_all | solution.py:191
  495.5 15.0 copy-start.70
  522.8 52.2 %all-to-all-start.4 = ((bf16[2,128,4096]{1,0,2:T(2,128)(2,1)}), bf16[2,128,4096]{1,0,2:T(2,128)(2,1)}, u32[]{:S(2)}, u32[]{:S(2)}) async-start(bf16[2,128,4096]{1,0,2:T(2,128)(2,1)} %copy.498), calls=%async_computation.4 | async-start | bytes 4194304 | tf_op jit(solution)/shard_map/all_to_all | solution.py:223
  527.2 376.0 %reduce-scatter.10.cloned.1.call-start = ((), (), s32[]{:S(2)}) async-start(), calls=%async_computation.17 | async-start | bytes 1179648
  596.0 35.0 %copy-start.9 = (f32[2,4,256,8,64]{2,4,3,1,0:T(8,128)}, f32[2,4,256,8,64]{2,4,3,1,0:T(8,128)S(1)}, u32[]{:S(2)}) copy-start(f32[2,4,256,8,64]{2,4,3,1,0:T(8,128)S(1)} %get-tuple-element.433) | copy-start | bytes 12582916
  596.0 29.8 %copy-start.14 = (f32[2,1024,128]{2,1,0:T(8,128)S(1)}, f32[2,1024,128]{2,1,0:T(8,128)}, u32[]{:S(2)}) copy-start(f32[2,1024,128]{2,1,0:T(8,128)} %copy-done.13) | copy-start | bytes 3145732
  649.3 15.0 copy-start.59
  745.3 299.0 %reduce-scatter.8.cloned.1.call-start = ((), (), s32[]{:S(2)}) async-start(), calls=%async_computation.16 | async-start | bytes 41943040 | tf_op jit(solution)/shard_map/reduce_scatter | solution.py:207
  765.0 26.5 %copy-start.37 = (f32[2,4,8]{2,1,0:T(4,128)S(1)}, f32[2,4,8]{2,1,0:T(4,128)}, u32[]{:S(2)}) copy-start(f32[2,4,8]{2,1,0:T(4,128)} %copy-done.36) | copy-start | bytes 772
  765.0 26.8 %copy-start.60 = (f32[4,2,8]{2,0,1:T(4,128)S(1)}, f32[4,2,8]{2,0,1:T(4,128)}, u32[]{:S(2)}) copy-start(f32[4,2,8]{2,0,1:T(4,128)} %copy-done.59) | copy-start | bytes 772
  765.0 26.9 %copy-start.40 = (f32[2,4,8,256]{3,2,1,0:T(8,128)S(1)}, f32[2,4,8,256]{3,2,1,0:T(8,128)}, u32[]{:S(2)}) copy-start(f32[2,4,8,256]{3,2,1,0:T(8,128)} %get-tuple-element.380) | copy-start | bytes 196612
  814.0 29.6 %all-to-all-start.7 = ((bf16[8,2,1024]{2,1,0:T(2,128)(2,1)}), bf16[8,2,1024]{2,1,0:T(2,128)(2,1)S(1)}, u32[]{:S(2)}, u32[]{:S(2)}) async-start(bf16[8,2,1024]{2,1,0:T(2,128)(2,1)} %reshape.438), calls=%async_computation.7 | async-start | bytes 65536 | tf_op jit(solution)/shard_map/all_to_all | solution.py:250
  843.6 54.1 %all-to-all-start.6 = ((bf16[2,1024,512]{2,0,1:T(2,128)(2,1)}), bf16[2,1024,512]{2,0,1:T(2,128)(2,1)}, u32[]{:S(2)}, u32[]{:S(2)}) async-start(bf16[2,1024,512]{2,0,1:T(2,128)(2,1)} %copy.517), calls=%async_computation.6 | async-start | bytes 4194304 | tf_op jit(solution)/shard_map/all_to_all | solution.py:243
  897.7 52.2 %all-to-all-start.5 = ((bf16[2,1024,512]{2,0,1:T(2,128)(2,1)}), bf16[2,1024,512]{2,0,1:T(2,128)(2,1)}, u32[]{:S(2)}, u32[]{:S(2)}) async-start(bf16[2,1024,512]{2,0,1:T(2,128)(2,1)} %copy.501), calls=%async_computation.5 | async-start | bytes 4194304 | tf_op jit(solution)/shard_map/all_to_all | solution.py:240
  902.0 613.3 %reduce-scatter.6.cloned.1.call-start = ((), (), s32[]{:S(2)}) async-start(), calls=%async_computation.14 | async-start | bytes 87162880 | tf_op jit(solution)/shard_map/reduce_scatter | solution.py:275
  907.8 47.0 %copy-start.26 = (bf16[32,8,8,512]{3,1,2,0:T(8,128)(2,1)}, bf16[32,8,8,512]{3,1,2,0:T(8,128)(2,1)S(1)}, u32[]{:S(2)}) copy-start(bf16[32,8,8,512]{3,1,2,0:T(8,128)(2,1)S(1)} %copy.597) | copy-start | bytes 6291460
  983.1 656.3 %all-reduce.19.cloned.1.call-start = ((), (), s32[]{:S(2)}) async-start(), calls=%async_computation.15 | async-start | bytes 139264 | tf_op jit(solution)/shard_map/psum | solution.py:292
  984.6 1427.2 %all-reduce.21.cloned.1.call-start = ((), (), s32[]{:S(2)}) async-start(), calls=%async_computation.18 | async-start | bytes 51642368 | tf_op jit(solution)/shard_map/psum | solution.py:291
  1530.5 18.1 copy-start.57
  (72 other events, 511.8 us)
Sparse Core Ops, SparseCore 0:
  9.6 213.9 all-gather.3
  247.6 67.1 all-gather.5
  316.4 104.4 all-gather.7
  745.5 62.2 reduce-scatter.9
  810.4 233.8 reduce-scatter.7
  1047.0 468.2 reduce-scatter.5
  1521.5 117.8 all-reduce.18
  1643.8 767.9 all-reduce.20
where the time goes:
time: 2440 us
  waiting for transfers between devices  1780 us (73%)
  matrix products  219 us (9%)
  local copies, waits for them, and re-layouts  179 us (7%)
  other arithmetic  166 us (7%)
  blocking collectives  40.5 us (2%)
  starting transfers between devices  38.5 us (2%)
    psum x1, waiting for transfers between devices, body(): lax.psum((in_weight_grad, out_weight_grad), 'seq')  772 us
    reduce_scatter x1, waiting for transfers between devices, body(): lax.psum_scatter(lax.dot_general(columns, proj_rows, (((0,), (0,)), ((),...  471 us
    all_gather x1, waiting for transfers between devices, body(): lax.all_gather(in_weight, 'wa', axis=0, tiled=True)  213 us
    another operation x14, other arithmetic  71.1 us
    dot_general x3, matrix products, block_chain(): jnp.einsum('sbhij,sbjhp->sbihp', weights, x_blocks, precision=HIGH)  65 us
    reduce_scatter x1, waiting for transfers between devices, body(): lax.psum_scatter(lax.dot_general(columns, branch_grad, (((0,), (0,)), (()...  59.7 us
    unnamed x184, local copies, waits for them, and re-layouts  53.7 us
  transfers between devices with their start and end apart: 16, of which 11 were waited for; matrix products, arithmetic and copies ran while one was open for 13% of the time, Pallas kernels for 0%

commit v1 on v0

--- a/solution.py
+++ b/solution.py
@@ -290,16 +290,19 @@
     token_grad = token_grad + cot_rows.astype(jnp.float32)
     in_weight_grad, out_weight_grad = lax.psum((in_weight_grad, out_weight_grad), "seq")
     small_grads = lax.psum(
-        (
-            norm_gain_grad,
-            conv_weight_grad,
-            conv_bias_grad,
-            dt_bias_grad,
-            a_log_grad,
-            skip_grad,
-            out_gain_grad,
-        ),
-        ("seq", "wa"),
+        lax.psum(
+            (
+                norm_gain_grad,
+                conv_weight_grad,
+                conv_bias_grad,
+                dt_bias_grad,
+                a_log_grad,
+                skip_grad,
+                out_gain_grad,
+            ),
+            "wa",
+        ),
+        "seq",
     )
     return (
         mixed_out,

time: 2440 us -> 2360 us (0.967)
  waiting for transfers between devices: 1780 us -> 1680 us
    psum x1, waiting for transfers between devices: 772 us -> 686 us  [body(): lax.psum((in_weight_grad, out_weight_grad), 'seq')]
    psum x1, waiting for transfers between devices: 46.6 us -> 0.02 us  [body(): lax.psum((norm_gain_grad, conv_weight_grad, conv_bias_grad, dt_bias_grad,...]
    psum x0 -> x1, blocking collectives: none -> 40.7 us  [body(): lax.psum(lax.psum((norm_gain_grad, conv_weight_grad, conv_bias_grad, dt_b...]
    reduce_scatter x1, waiting for transfers between devices: 59.7 us -> 98.3 us  [body(): lax.psum_scatter(lax.dot_general(columns, branch_grad, (((0,), (0,)), (()...]
    psum x1, blocking collectives: 40.5 us -> 11.4 us  [body(): lax.psum((norm_gain_grad, conv_weight_grad, conv_bias_grad, dt_bias_grad,...]
    unnamed x184 -> x186, local copies, waits for them, and re-layouts: 53.7 us -> 53.1 us
  transfers between devices with their start and end apart: 16 -> 16, of which waited for: 11 -> 10; matrix products, arithmetic and copies ran while one was open for 13% -> 13% of each run, Pallas kernels for 0% -> 0%
where the time goes in v1:
time: 2360 us; the launch traced here: 2350 us
  waiting for transfers between devices  1680 us (71%)
  matrix products  220 us (9%)
  local copies, waits for them, and re-layouts  177 us (8%)
  other arithmetic  161 us (7%)
  blocking collectives  52.1 us (2%)
  starting transfers between devices  39.1 us (2%)
    psum x1, waiting for transfers between devices, body(): lax.psum((in_weight_grad, out_weight_grad), 'seq')  686 us
    reduce_scatter x1, waiting for transfers between devices, body(): lax.psum_scatter(lax.dot_general(columns, proj_rows, (((0,), (0,)), ((),...  471 us
    all_gather x1, waiting for transfers between devices, body(): lax.all_gather(in_weight, 'wa', axis=0, tiled=True)  213 us
    reduce_scatter x1, waiting for transfers between devices, body(): lax.psum_scatter(lax.dot_general(columns, branch_grad, (((0,), (0,)), (()...  98.3 us
    another operation x14, other arithmetic  65.4 us
    dot_general x3, matrix products, block_chain(): jnp.einsum('sbhij,sbjhp->sbihp', weights, x_blocks, precision=HIGH)  64.8 us
    unnamed x186, local copies, waits for them, and re-layouts  53.1 us
  transfers between devices with their start and end apart: 16, of which 10 were waited for; matrix products, arithmetic and copies ran while one was open for 13% of the time, Pallas kernels for 0%

profile of v1, /device:TPU:0, one launch (start us, length us, event | category | flops | bytes accessed | tf_op | source)
XLA Modules:
  0.0 2349.2 jit_solution(12366420811468137577)
XLA Ops:
  10.1 213.5 %all-gather.4.cloned.1.call-done = bf16[2048,8512]{0,1:T(8,128)(2,1)} async-done(((bf16[512,8512]{0,1:T(8,128)(2,1)}), bf16[2048,8512]{0,1:T(8,128)(2,1)}) %all-gather.4.cloned.1.call-update) | async-done | bytes 34865168 | tf_op jit(solution)/shard_map/all_gather | solution.py:121
  223.6 15.1 convolution_convert_fusion
  277.8 43.5 %all-to-all-done = bf16[2,128,4096]{1,0,2:T(2,128)(2,1)S(1)} async-done(((bf16[2,128,4096]{1,0,2:T(2,128)(2,1)}), bf16[2,128,4096]{1,0,2:T(2,128)(2,1)S(1)}, u32[]{:S(2)}, u32[]{:S(2)}) %all-to-all-start) | async-done | bytes 2097184 | tf_op jit(solution)/shard_map/all_to_all | solution.py:135
  334.8 7.5 fusion.24
  376.8 19.7 bitcast_add_fusion.3
  433.1 44.0 %all-to-all-done.3 = bf16[2,1024,512]{2,0,1:T(2,128)(2,1)} async-done(((bf16[2,1024,512]{2,0,1:T(2,128)(2,1)}), bf16[2,1024,512]{2,0,1:T(2,128)(2,1)}, u32[]{:S(2)}, u32[]{:S(2)}) %all-to-all-start.3) | async-done | bytes 2097184 | tf_op jit(solution)/shard_map/all_to_all | solution.py:191
  495.6 15.1 multiply_reduce_fusion.7
  527.5 6.7 copy.494
  540.0 35.3 %all-to-all-done.4 = bf16[2,128,4096]{1,0,2:T(2,128)(2,1)} async-done(((bf16[2,128,4096]{1,0,2:T(2,128)(2,1)}), bf16[2,128,4096]{1,0,2:T(2,128)(2,1)}, u32[]{:S(2)}, u32[]{:S(2)}) %all-to-all-start.4) | async-done | bytes 2097184 | tf_op jit(solution)/shard_map/all_to_all | solution.py:223
  589.7 6.5 multiply_reduce_fusion.9
  596.3 29.8 %fusion.9 = (f32[2,4,8,256]{3,2,1,0:T(8,128)S(1)}, f32[2,4,8,256]{3,2,1,0:T(8,128)S(1)}, f32[2,4,8,256]{3,2,1,0:T(8,128)}, f32[2,4,256,256]{3,2,1,0:T(8,128)}) fusion(f32[2,4,8,256]{3,2,1,0:T(8,128)S(1)} %get-tuple-element.446, f32[2,4,8,256]{3,2,1,0:T(8,128)S(1)} %get-tuple-element.444, f32[2,4,256,256]{3,2,1,0:T(8,128)S(1)} %copy-done.32, ...), kind=kOutput, calls=%fused_computation.21 | convolution fusion | flops 3283566592 | bytes 12976128 | tf_op jit(solution)/shard_map/transpose(jvp(sbhij,sbjhp->sbihp))/dot_general | solution.py:40
  631.3 7.8 fusion.90
  640.7 9.1 while.35
  649.8 10.8 fusion.85
  664.8 15.3 bitcast_add_fusion.2
  704.9 10.8 multiply_reduce_fusion.8
  716.9 10.7 multiply_reduce_fusion.4
  753.9 14.6 fusion.136
  774.5 19.8 reduce-window.34
  795.5 19.8 reduce-window.36
  821.0 11.1 add_convert_fusion
  850.7 43.9 %all-to-all-done.6 = bf16[2,1024,512]{2,0,1:T(2,128)(2,1)} async-done(((bf16[2,1024,512]{2,0,1:T(2,128)(2,1)}), bf16[2,1024,512]{2,0,1:T(2,128)(2,1)}, u32[]{:S(2)}, u32[]{:S(2)}) %all-to-all-start.6) | async-done | bytes 2097184 | tf_op jit(solution)/shard_map/all_to_all | solution.py:243
  905.0 41.9 %all-to-all-done.5 = bf16[2,1024,512]{2,0,1:T(2,128)(2,1)} async-done(((bf16[2,1024,512]{2,0,1:T(2,128)(2,1)}), bf16[2,1024,512]{2,0,1:T(2,128)(2,1)}, u32[]{:S(2)}, u32[]{:S(2)}) %all-to-all-start.5) | async-done | bytes 2097184 | tf_op jit(solution)/shard_map/all_to_all | solution.py:240
  951.8 28.2 %fusion.95 = f32[2048,8512]{0,1:T(8,128)} fusion(bf16[256,2048]{1,0:T(8,128)(2,1)} %copy-done.29, bf16[256,64]{1,0:T(8,128)(2,1)S(1)} %copy.528, bf16[256,256]{1,0:T(8,128)(2,1)S(1)} %bitcast.400, bf16[256,4096]{1,0:T(8,128)(2,1)S(1)} %bitcast.377, bf16[256,4096]{1,0:T(8,128)(2,1)} %bitcast.379), kind=kOutput, calls=%fused_computation.140 | convolution fusion | flops 8942911488 | bytes 75137024 | tf_op jit(solution)/shard_map/dot_general | solution.py:276
  980.3 98.3 %reduce-scatter.8.cloned.1.call-done = f32[1024,2048]{1,0:T(8,128)} async-done(((f32[4096,2048]{1,0:T(8,128)}), f32[1024,2048]{1,0:T(8,128)}) %reduce-scatter.8.cloned.1.call-update) | async-done | bytes 8388624 | tf_op jit(solution)/shard_map/reduce_scatter | solution.py:207
  1078.6 470.9 %reduce-scatter.6.cloned.1.call-done = f32[512,8512]{0,1:T(8,128)} async-done(((f32[2048,8512]{0,1:T(8,128)}), f32[512,8512]{0,1:T(8,128)}) %reduce-scatter.6.cloned.1.call-update) | async-done | bytes 17432592 | tf_op jit(solution)/shard_map/reduce_scatter | solution.py:275
  1550.8 12.6 fusion.49
  1564.6 18.2 fusion.58
  1582.7 11.4 all-reduce.16
  1594.1 40.7 %all-reduce.14 = (f32[2048]{0:T(1024)}, f32[4352]{0:T(1024)}, f32[64]{0:T(128)}, f32[64]{0:T(128)}, f32[64]{0:T(128)}, /*index=5*/f32[4096]{0:T(1024)}) all-reduce(f32[2048]{0:T(1024)S(1)} %get-tuple-element.430, f32[4352]{0:T(1024)S(1)} %get-tuple-element.431, ...), channel_id=1, replica_groups=mesh['seq'=8,'wa'=4] {'seq'}, use_global_device_ids=true, to_apply=%region_26.27 | all-reduce | flops 10688 | bytes 85504 | tf_op jit(solution)/shard_map/psum | solution.py:292
  1638.4 686.3 %all-reduce.22.cloned.1.call-done = (f32[512,8512]{0,1:T(8,128)}, f32[4,4352]{1,0:T(4,128)}, f32[1024,2048]{1,0:T(8,128)}) async-done(((f32[512,8512]{0,1:T(8,128)}, f32[4,4352]{1,0:T(4,128)}, f32[1024,2048]{1,0:T(8,128)}), (f32[512,8512]{0,1:T(8,128)}, f32[4,4352]{1,0:T(4,128)}, f32[1024,2048]{1,0:T(8,128)})) %all-reduce.22.cloned.1.call-update) | async-done | bytes 25890832 | tf_op jit(solution)/shard_map/psum | solution.py:291
  2324.7 13.4 copy.712
  (400 shorter events, 314.9 us)
Async XLA Ops:
  7.2 216.4 %all-gather.4.cloned.1.call-start = ((), (), s32[]{:S(2)}) async-start(), calls=%async_computation.11 | async-start | bytes 43581440 | tf_op jit(solution)/shard_map/all_gather | solution.py:121
  7.9 324.1 %all-gather.6.cloned.1.call-start = ((), (), s32[]{:S(2)}) async-start(), calls=%async_computation.12 | async-start | bytes 1179648 | tf_op jit(solution)/shard_map/all_gather | solution.py:138
  10.1 228.5 %copy-start.29 = (bf16[256,2048]{1,0:T(8,128)(2,1)}, bf16[256,2048]{1,0:T(8,128)(2,1)S(1)}, u32[]{:S(2)}) copy-start(bf16[256,2048]{1,0:T(8,128)(2,1)S(1)} %fusion.52) | copy-start | bytes 3145732
  247.5 248.0 %all-gather.8.cloned.1.call-start = ((), (), s32[]{:S(2)}) async-start(), calls=%async_computation.13 | async-start | bytes 20971520 | tf_op jit(solution)/shard_map/all_gather | solution.py:200
  248.9 12.2 all-to-all-start.1
  261.1 60.2 %all-to-all-start = ((bf16[2,128,4096]{1,0,2:T(2,128)(2,1)}), bf16[2,128,4096]{1,0,2:T(2,128)(2,1)S(1)}, u32[]{:S(2)}, u32[]{:S(2)}) async-start(bf16[2,128,4096]{1,0,2:T(2,128)(2,1)} %slice.142), calls=%async_computation | async-start | bytes 4194304 | tf_op jit(solution)/shard_map/all_to_all | solution.py:135
  265.1 146.7 %copy-start.52 = (f32[512]{0:T(512)}, f32[512]{0:T(512)S(1)}, u32[]{:S(2)}) copy-start(f32[512]{0:T(512)S(1)} %mul.518) | copy-start | bytes 6148
  265.2 69.6 %copy-start.41 = (f32[768]{0:T(1024)}, f32[768]{0:T(1024)S(1)}, u32[]{:S(2)}) copy-start(f32[768]{0:T(1024)S(1)} %get-tuple-element.391) | copy-start | bytes 9220
  265.2 69.6 %copy-start.43 = (f32[768]{0:T(1024)}, f32[768]{0:T(1024)S(1)}, u32[]{:S(2)}) copy-start(f32[768]{0:T(1024)S(1)} %get-tuple-element.392) | copy-start | bytes 9220
  265.2 69.6 %copy-start.45 = (f32[768]{0:T(1024)}, f32[768]{0:T(1024)S(1)}, u32[]{:S(2)}) copy-start(f32[768]{0:T(1024)S(1)} %get-tuple-element.393) | copy-start | bytes 9220
  265.2 69.6 %copy-start.47 = (f32[768]{0:T(1024)}, f32[768]{0:T(1024)S(1)}, u32[]{:S(2)}) copy-start(f32[768]{0:T(1024)S(1)} %get-tuple-element.394) | copy-start | bytes 9220
  277.6 51.2 %copy-start.36 = (f32[2,4,8]{2,1,0:T(4,128)}, f32[2,4,8]{2,1,0:T(4,128)S(1)}, u32[]{:S(2)}) copy-start(f32[2,4,8]{2,1,0:T(4,128)S(1)} %slice_reduce_fusion.2) | copy-start | bytes 772
  321.3 85.8 %all-to-all-start.2 = ((bf16[2,128,4096]{1,0,2:T(2,128)(2,1)}), bf16[2,128,4096]{1,0,2:T(2,128)(2,1)}, u32[]{:S(2)}, u32[]{:S(2)}) async-start(bf16[2,128,4096]{1,0,2:T(2,128)(2,1)} %reshape.388), calls=%async_computation.2 | async-start | bytes 4194304 | tf_op jit(solution)/shard_map/all_to_all | solution.py:134
  424.1 53.0 %all-to-all-start.3 = ((bf16[2,1024,512]{2,0,1:T(2,128)(2,1)}), bf16[2,1024,512]{2,0,1:T(2,128)(2,1)}, u32[]{:S(2)}, u32[]{:S(2)}) async-start(bf16[2,1024,512]{2,0,1:T(2,128)(2,1)} %copy.495), calls=%async_computation.3 | async-start | bytes 4194304 | tf_op jit(solution)/shard_map/all_to_all | solution.py:191
  495.5 15.2 copy-start.70
  523.1 52.2 %all-to-all-start.4 = ((bf16[2,128,4096]{1,0,2:T(2,128)(2,1)}), bf16[2,128,4096]{1,0,2:T(2,128)(2,1)}, u32[]{:S(2)}, u32[]{:S(2)}) async-start(bf16[2,128,4096]{1,0,2:T(2,128)(2,1)} %copy.498), calls=%async_computation.4 | async-start | bytes 4194304 | tf_op jit(solution)/shard_map/all_to_all | solution.py:223
  527.4 372.9 %reduce-scatter.10.cloned.1.call-start = ((), (), s32[]{:S(2)}) async-start(), calls=%async_computation.17 | async-start | bytes 1179648
  596.3 35.1 %copy-start.9 = (f32[2,4,256,8,64]{2,4,3,1,0:T(8,128)}, f32[2,4,256,8,64]{2,4,3,1,0:T(8,128)S(1)}, u32[]{:S(2)}) copy-start(f32[2,4,256,8,64]{2,4,3,1,0:T(8,128)S(1)} %get-tuple-element.440) | copy-start | bytes 12582916
  596.3 29.8 %copy-start.14 = (f32[2,1024,128]{2,1,0:T(8,128)S(1)}, f32[2,1024,128]{2,1,0:T(8,128)}, u32[]{:S(2)}) copy-start(f32[2,1024,128]{2,1,0:T(8,128)} %copy-done.13) | copy-start | bytes 3145732
  649.8 15.0 copy-start.59
  745.7 234.7 %all-reduce.20.cloned.1.call-start = ((), (), s32[]{:S(2)}) async-start(), calls=%async_computation.15 | async-start | bytes 139264 | tf_op jit(solution)/shard_map/psum | solution.py:293
  753.8 324.8 %reduce-scatter.8.cloned.1.call-start = ((), (), s32[]{:S(2)}) async-start(), calls=%async_computation.16 | async-start | bytes 41943040 | tf_op jit(solution)/shard_map/reduce_scatter | solution.py:207
  768.4 26.5 %copy-start.37 = (f32[2,4,8]{2,1,0:T(4,128)S(1)}, f32[2,4,8]{2,1,0:T(4,128)}, u32[]{:S(2)}) copy-start(f32[2,4,8]{2,1,0:T(4,128)} %copy-done.36) | copy-start | bytes 772
  768.4 26.8 %copy-start.60 = (f32[4,2,8]{2,0,1:T(4,128)S(1)}, f32[4,2,8]{2,0,1:T(4,128)}, u32[]{:S(2)}) copy-start(f32[4,2,8]{2,0,1:T(4,128)} %copy-done.59) | copy-start | bytes 772
  768.5 26.9 %copy-start.40 = (f32[2,4,8,256]{3,2,1,0:T(8,128)S(1)}, f32[2,4,8,256]{3,2,1,0:T(8,128)}, u32[]{:S(2)}) copy-start(f32[2,4,8,256]{3,2,1,0:T(8,128)} %get-tuple-element.380) | copy-start | bytes 196612
  817.4 23.3 all-to-all-start.7
  840.7 54.0 %all-to-all-start.6 = ((bf16[2,1024,512]{2,0,1:T(2,128)(2,1)}), bf16[2,1024,512]{2,0,1:T(2,128)(2,1)}, u32[]{:S(2)}, u32[]{:S(2)}) async-start(bf16[2,1024,512]{2,0,1:T(2,128)(2,1)} %copy.517), calls=%async_computation.6 | async-start | bytes 4194304 | tf_op jit(solution)/shard_map/all_to_all | solution.py:243
  894.7 52.2 %all-to-all-start.5 = ((bf16[2,1024,512]{2,0,1:T(2,128)(2,1)}), bf16[2,1024,512]{2,0,1:T(2,128)(2,1)}, u32[]{:S(2)}, u32[]{:S(2)}) async-start(bf16[2,1024,512]{2,0,1:T(2,128)(2,1)} %copy.501), calls=%async_computation.5 | async-start | bytes 4194304 | tf_op jit(solution)/shard_map/all_to_all | solution.py:240
  899.0 650.5 %reduce-scatter.6.cloned.1.call-start = ((), (), s32[]{:S(2)}) async-start(), calls=%async_computation.14 | async-start | bytes 87162880 | tf_op jit(solution)/shard_map/reduce_scatter | solution.py:275
  905.0 46.9 %copy-start.26 = (bf16[32,8,8,512]{3,1,2,0:T(8,128)(2,1)}, bf16[32,8,8,512]{3,1,2,0:T(8,128)(2,1)S(1)}, u32[]{:S(2)}) copy-start(bf16[32,8,8,512]{3,1,2,0:T(8,128)(2,1)S(1)} %copy.597) | copy-start | bytes 6291460
  980.1 1344.7 %all-reduce.22.cloned.1.call-start = ((), (), s32[]{:S(2)}) async-start(), calls=%async_computation.18 | async-start | bytes 51781632 | tf_op jit(solution)/shard_map/psum | solution.py:291
  1564.6 18.2 copy-start.57
  (73 other events, 533.1 us)
Sparse Core Ops, SparseCore 0:
  9.6 213.9 all-gather.3
  247.6 67.1 all-gather.5
  316.4 104.4 all-gather.7
  745.8 62.4 reduce-scatter.9
  811.2 28.1 all-reduce.19
  841.8 236.7 reduce-scatter.7
  1081.3 468.2 reduce-scatter.5
  1555.2 769.5 all-reduce.21
